TPU v7x, 32 devices: a whole 2x2x4 slice. The times are simulated.
32 devices in a mesh: batch: 4 (over x, core), head: 8 (over z, y).
Axes of the slice: x: 2, y: 2, z: 4, core: 2. Of those that a mesh axis runs over, the one named last changes fastest.
Arguments:
- tokens: bfloat16 [5120, 2048], P('batch'), may hold values from -6 to 6
- segment_ids: int32 [5120], P('batch'), may hold values from 0 to 6, as said below
- norm1_gain: bfloat16 [2048], P('batch'), may hold values from 0.25 to 1.75
- w_query: bfloat16 [2048, 1024], P('batch', 'head'), may hold values from -0.125 to 0.125
- w_key: bfloat16 [2048, 512], P('batch', 'head'), may hold values from -0.125 to 0.125
- w_value: bfloat16 [2048, 512], P('batch', 'head'), may hold values from -0.125 to 0.125
- w_gate: bfloat16 [2048, 1024], P('batch', 'head'), may hold values from -0.125 to 0.125
- w_out: bfloat16 [1024, 2048], P('head', 'batch'), may hold values from -4 to 4
- norm2_gain: bfloat16 [2048], P('batch'), may hold values from 0.25 to 1.75
- w_mlp_gate: bfloat16 [2048, 6144], P('batch', 'head'), may hold values from -0.125 to 0.125
- w_mlp_up: bfloat16 [2048, 6144], P('batch', 'head'), may hold values from -0.125 to 0.125
- w_down: bfloat16 [6144, 2048], P('head', 'batch'), may hold values from -0.078125 to 0.078125
- out_grad: bfloat16 [5120, 2048], P('batch'), may hold values from -6 to 6
Outputs:
- output: bfloat16 [5120, 2048], P('batch')
- d_tokens: bfloat16 [5120, 2048], P('batch')
- d_norm1_gain: float32 [2048], P('batch')
- d_w_query: float32 [2048, 1024], P('batch', 'head')
- d_w_key: float32 [2048, 512], P('batch', 'head')
- d_w_value: float32 [2048, 512], P('batch', 'head')
- d_w_gate: float32 [2048, 1024], P('batch', 'head')
- d_w_out: float32 [1024, 2048], P('head', 'batch')
- d_norm2_gain: float32 [2048], P('batch')
- d_w_mlp_gate: float32 [2048, 6144], P('batch', 'head')
- d_w_mlp_up: float32 [2048, 6144], P('batch', 'head')
- d_w_down: float32 [6144, 2048], P('head', 'batch')
Inputs may be any that keep to these rules, and one draw needn't show every extreme that they name: `segment_ids`: segment ids never fall along the packed batch and every id from 0 to 6 occurs.
All inputs are finite; a program needn't handle non-finite values.
Results may differ from a plain program's by a relative error of at most 0.02.
Values may be sent and summed in bfloat16 or wider, within the bound.
A program may use at most 256 MiB of HBM per device.

v0:
```python
import math
import jax
import jax.numpy as jnp
from jax import lax
from jax.sharding import PartitionSpec as P

EPSILON = 1e-06
MASKED = -1e30


def from_partner(block, axis, stride):
    count = lax.axis_size(axis)
    route = []
    for low in range(count):
        high = low | 1 << stride
        if high != low and high < count:
            route += [(low, high), (high, low)]
    return lax.ppermute(block, axis, route)


def matmul(left, right):
    return jnp.dot(left, right, preferred_element_type=jnp.float32)


def rows_inner(left, right):
    return lax.dot_general(
        left, right, (((0,), (0,)), ((), ())), preferred_element_type=jnp.float32
    )


def cols_inner(left, right):
    return lax.dot_general(
        left, right, (((1,), (1,)), ((), ())), preferred_element_type=jnp.float32
    )


def rms_scale(values):
    return lax.rsqrt(jnp.mean(values * values, axis=1, keepdims=True) + EPSILON)


def keep_same(state):
    return state


def per_device(
    tokens,
    segment_ids,
    norm1_gain,
    w_query,
    w_key,
    w_value,
    w_gate,
    w_out,
    norm2_gain,
    w_mlp_gate,
    w_mlp_up,
    w_down,
    out_grad,
):
    gathered = (
        lax.all_gather(norm1_gain, "batch", axis=0, tiled=True),
        lax.all_gather(w_query, "batch", axis=0, tiled=True),
        lax.all_gather(w_key, "batch", axis=0, tiled=True),
        lax.all_gather(w_value, "batch", axis=0, tiled=True),
        lax.all_gather(w_gate, "batch", axis=0, tiled=True),
        lax.all_gather(w_out, "batch", axis=1, tiled=True),
        lax.all_gather(norm2_gain, "batch", axis=0, tiled=True),
        lax.all_gather(w_mlp_gate, "batch", axis=0, tiled=True),
        lax.all_gather(w_mlp_up, "batch", axis=0, tiled=True),
        lax.all_gather(w_down, "batch", axis=1, tiled=True),
    )
    (
        gain_one,
        query_full,
        key_full,
        value_full,
        gate_full,
        out_full,
        gain_two,
        mgate_full,
        mup_full,
        down_full,
    ) = gathered
    gain_one = gain_one.astype(jnp.float32)
    gain_two = gain_two.astype(jnp.float32)
    row_count = tokens.shape[0]
    head_size = query_full.shape[1]
    half_width = key_full.shape[1]
    scale_factor = 1.0 / math.sqrt(head_size)
    positions = lax.axis_index("batch") * row_count + jnp.arange(row_count, dtype=jnp.int32)
    inputs = tokens.astype(jnp.float32)
    recip_one = rms_scale(inputs)
    normed_one = (inputs * recip_one * gain_one).astype(jnp.bfloat16)
    queries = matmul(normed_one, query_full).astype(jnp.bfloat16)
    kv_half = matmul(normed_one, jnp.concatenate([key_full, value_full], axis=1)).astype(
        jnp.bfloat16
    )
    partner = from_partner(kv_half, "head", 0)
    lower_half = lax.axis_index("head") % 2 == 0
    own_key, own_value = (kv_half[:, :half_width], kv_half[:, half_width:])
    mate_key, mate_value = (partner[:, :half_width], partner[:, half_width:])
    keys_full = jnp.where(
        lower_half, jnp.concatenate([own_key, mate_key], 1), jnp.concatenate([mate_key, own_key], 1)
    )
    values_full = jnp.where(
        lower_half,
        jnp.concatenate([own_value, mate_value], 1),
        jnp.concatenate([mate_value, own_value], 1),
    )
    kv_local = jnp.concatenate([keys_full, values_full], axis=1)
    kv_all, seg_all = (
        lax.all_gather(kv_local, "batch", axis=0, tiled=True),
        lax.all_gather(segment_ids, "batch", axis=0, tiled=True),
    )
    group_total = kv_all.shape[0] // row_count
    per_block = max(
        (
            step
            for step in range(1, group_total + 1)
            if group_total % step == 0 and step * row_count <= max(row_count, 1024)
        )
    )
    block_rows = per_block * row_count
    block_total = group_total // per_block

    def block_parts(block_index):
        first_row = block_index * block_rows
        key_block = kv_all[first_row : first_row + block_rows, :head_size]
        value_block = kv_all[first_row : first_row + block_rows, head_size:]
        seg_block = seg_all[first_row : first_row + block_rows]
        key_pos = first_row + jnp.arange(block_rows, dtype=jnp.int32)
        allowed = (segment_ids[:, None] == seg_block[None, :]) & (
            key_pos[None, :] <= positions[:, None]
        )
        scores = cols_inner(queries, key_block) * scale_factor
        return (scores, allowed, key_block, value_block)

    def is_live(block_index):
        first_row = block_index * block_rows
        return (first_row <= positions[-1]) & (
            seg_all[first_row + block_rows - 1] >= segment_ids[0]
        )

    run_max = jnp.full((row_count,), MASKED, jnp.float32)
    run_sum = jnp.zeros((row_count,), jnp.float32)
    for block_index in range(block_total):

        def grow(state, block_index=block_index):
            old_max, old_sum = state
            scores, allowed, key_block, value_block = block_parts(block_index)
            new_max = jnp.maximum(old_max, jnp.max(jnp.where(allowed, scores, MASKED), axis=1))
            weights = jnp.where(allowed, jnp.exp(scores - new_max[:, None]), 0.0)
            return (new_max, old_sum * jnp.exp(old_max - new_max) + jnp.sum(weights, axis=1))

        run_max, run_sum = lax.cond(is_live(block_index), grow, keep_same, (run_max, run_sum))
    log_total = run_max + jnp.log(run_sum)

    def probs_of(block_index):
        scores, allowed, key_block, value_block = block_parts(block_index)
        return (
            jnp.where(allowed, jnp.exp(scores - log_total[:, None]), 0.0),
            key_block,
            value_block,
        )

    attended = jnp.zeros((row_count, head_size), jnp.float32)
    for block_index in range(block_total):

        def accumulate(running, block_index=block_index):
            probs, key_block, value_block = probs_of(block_index)
            return running + matmul(probs.astype(jnp.bfloat16), value_block)

        attended = lax.cond(is_live(block_index), accumulate, keep_same, attended)
    gate_vals = jax.nn.sigmoid(matmul(normed_one, gate_full))
    mixed = (attended * gate_vals).astype(jnp.bfloat16)
    attn_part = matmul(mixed, out_full)
    resid = inputs + lax.psum(attn_part, "head")
    recip_two = rms_scale(resid)
    normed_two = (resid * recip_two * gain_two).astype(jnp.bfloat16)
    gate_pre = matmul(normed_two, mgate_full)
    up_pre = matmul(normed_two, mup_full)
    sig_gate = jax.nn.sigmoid(gate_pre)
    silu_gate = gate_pre * sig_gate
    hidden = (silu_gate * up_pre).astype(jnp.bfloat16)
    mlp_part = matmul(hidden, down_full)
    d_down = rows_inner(hidden, out_grad)
    d_hidden = cols_inner(out_grad, down_full)
    d_gate_pre = (d_hidden * up_pre * sig_gate * (1.0 + gate_pre * (1.0 - sig_gate))).astype(
        jnp.bfloat16
    )
    d_up_pre = (d_hidden * silu_gate).astype(jnp.bfloat16)
    d_mgate = rows_inner(normed_two, d_gate_pre)
    d_mup = rows_inner(normed_two, d_up_pre)
    dn2_part = cols_inner(d_gate_pre, mgate_full) + cols_inner(d_up_pre, mup_full)
    mlp_total = lax.psum(mlp_part.astype(jnp.bfloat16), "head").astype(jnp.float32)
    output = (resid + mlp_total).astype(jnp.bfloat16)
    d_normed_two = lax.psum(dn2_part.astype(jnp.bfloat16), "head").astype(jnp.float32)
    gain_two_full = jnp.sum(d_normed_two * resid * recip_two, axis=0)
    gain_two_term = jnp.where(
        lax.axis_index("head") == 0, gain_two_full, jnp.zeros_like(gain_two_full)
    )
    weighted_two = gain_two * d_normed_two
    d_resid = (
        out_grad.astype(jnp.float32)
        + recip_two * weighted_two
        - resid * recip_two**3 * jnp.mean(weighted_two * resid, axis=1, keepdims=True)
    )
    d_resid_low = d_resid.astype(jnp.bfloat16)
    d_out = rows_inner(mixed, d_resid_low)
    d_mixed = cols_inner(d_resid_low, out_full)
    d_attended = (d_mixed * gate_vals).astype(jnp.bfloat16)
    d_gate_logit = (d_mixed * attended * gate_vals * (1.0 - gate_vals)).astype(jnp.bfloat16)
    delta = jnp.zeros((row_count,), jnp.float32)
    for block_index in range(block_total):

        def delta_add(running, block_index=block_index):
            probs, key_block, value_block = probs_of(block_index)
            return running + jnp.sum(probs * cols_inner(d_attended, value_block), axis=1)

        delta = lax.cond(is_live(block_index), delta_add, keep_same, delta)
    d_queries = jnp.zeros((row_count, head_size), jnp.float32)
    grad_pieces = []
    for block_index in range(block_total):

        def block_grads(running, block_index=block_index):
            probs, key_block, value_block = probs_of(block_index)
            d_probs = cols_inner(d_attended, value_block)
            d_scores = (probs * (d_probs - delta[:, None]) * scale_factor).astype(jnp.bfloat16)
            d_key_block = rows_inner(d_scores, queries)
            d_value_block = rows_inner(probs.astype(jnp.bfloat16), d_attended)
            return (
                running + matmul(d_scores, key_block),
                jnp.concatenate([d_key_block, d_value_block], axis=1),
            )

        def block_empty(running):
            return (running, jnp.zeros((block_rows, 2 * head_size), jnp.float32))

        d_queries, grad_piece = lax.cond(is_live(block_index), block_grads, block_empty, d_queries)
        grad_pieces.append(grad_piece)
    d_kv_all = jnp.concatenate(grad_pieces, axis=0)
    d_kv_own = lax.psum_scatter(
        d_kv_all.astype(jnp.bfloat16), "batch", scatter_dimension=0, tiled=True
    ).astype(jnp.float32)
    d_kv_mate = from_partner(d_kv_own.astype(jnp.bfloat16), "head", 0).astype(d_kv_own.dtype)
    d_kv_low = (d_kv_own + d_kv_mate).astype(jnp.bfloat16)
    d_key_half = jnp.where(lower_half, d_kv_low[:, :half_width], d_kv_low[:, half_width:head_size])
    d_value_half = jnp.where(
        lower_half,
        d_kv_low[:, head_size : head_size + half_width],
        d_kv_low[:, head_size + half_width :],
    )
    d_queries_low = d_queries.astype(jnp.bfloat16)
    d_query_w = rows_inner(normed_one, d_queries_low)
    d_key_w = rows_inner(normed_one, d_key_half)
    d_value_w = rows_inner(normed_one, d_value_half)
    d_gate_w = rows_inner(normed_one, d_gate_logit)
    dn1_part = (
        cols_inner(d_queries_low, query_full)
        + cols_inner(d_key_half, key_full)
        + cols_inner(d_value_half, value_full)
        + cols_inner(d_gate_logit, gate_full)
    )
    d_normed_one, d_gain_two = (
        lax.psum(dn1_part.astype(jnp.bfloat16), "head").astype(jnp.float32),
        lax.psum(gain_two_term.astype(jnp.bfloat16), "head").astype(jnp.float32),
    )
    d_gain_one = jnp.sum(d_normed_one * inputs * recip_one, axis=0)
    weighted_one = gain_one * d_normed_one
    d_tokens = (
        d_resid
        + recip_one * weighted_one
        - inputs * recip_one**3 * jnp.mean(weighted_one * inputs, axis=1, keepdims=True)
    ).astype(jnp.bfloat16)
    summed = (
        lax.psum_scatter(
            d_gain_one.astype(jnp.bfloat16), "batch", scatter_dimension=0, tiled=True
        ).astype(jnp.float32),
        lax.psum_scatter(
            d_query_w.astype(jnp.bfloat16), "batch", scatter_dimension=0, tiled=True
        ).astype(jnp.float32),
        lax.psum_scatter(
            d_key_w.astype(jnp.bfloat16), "batch", scatter_dimension=0, tiled=True
        ).astype(jnp.float32),
        lax.psum_scatter(
            d_value_w.astype(jnp.bfloat16), "batch", scatter_dimension=0, tiled=True
        ).astype(jnp.float32),
        lax.psum_scatter(
            d_gate_w.astype(jnp.bfloat16), "batch", scatter_dimension=0, tiled=True
        ).astype(jnp.float32),
        lax.psum_scatter(
            d_out.astype(jnp.bfloat16), "batch", scatter_dimension=1, tiled=True
        ).astype(jnp.float32),
        lax.psum_scatter(
            d_gain_two.astype(jnp.bfloat16), "batch", scatter_dimension=0, tiled=True
        ).astype(jnp.float32),
        lax.psum_scatter(
            d_mgate.astype(jnp.bfloat16), "batch", scatter_dimension=0, tiled=True
        ).astype(jnp.float32),
        lax.psum_scatter(
            d_mup.astype(jnp.bfloat16), "batch", scatter_dimension=0, tiled=True
        ).astype(jnp.float32),
        lax.psum_scatter(
            d_down.astype(jnp.bfloat16), "batch", scatter_dimension=1, tiled=True
        ).astype(jnp.float32),
    )
    return (
        output,
        d_tokens,
        summed[0],
        summed[1],
        summed[2],
        summed[3],
        summed[4],
        summed[5],
        summed[6],
        summed[7],
        summed[8],
        summed[9],
    )


def solution(mesh):
    return jax.shard_map(
        per_device,
        mesh=mesh,
        in_specs=(
            P("batch", None),
            P("batch"),
            P("batch"),
            P("batch", "head"),
            P("batch", "head"),
            P("batch", "head"),
            P("batch", "head"),
            P("head", "batch"),
            P("batch"),
            P("batch", "head"),
            P("batch", "head"),
            P("head", "batch"),
            P("batch", None),
        ),
        out_specs=(
            P("batch", None),
            P("batch", None),
            P("batch"),
            P("batch", "head"),
            P("batch", "head"),
            P("batch", "head"),
            P("batch", "head"),
            P("head", "batch"),
            P("batch"),
            P("batch", "head"),
            P("batch", "head"),
            P("head", "batch"),
        ),
        check_vma=False,
    )
```

profile of v0, /device:TPU:0, one launch (start us, length us, event | category | flops | bytes accessed | tf_op | source)
XLA Modules:
  0.0 1581.4 jit_solution(1215481020769771091)
XLA Ops:
  38.2 8.3 collective-permute-done
  62.4 10.5 all_gather.41
  92.7 9.2 conditional.16
  124.7 57.2 %all-gather.2 = bf16[4,1,512]{2,1,0:T(2,128)(2,1)S(1)} all-gather(bf16[1,1,512]{2,1,0:T(2,128)(2,1)S(1)} %reshape.212), channel_id=1, replica_groups=mesh['batch'=4,'head'=8] {'batch'}, dimensions={0}, use_global_device_ids=true | all-gather | bytes 5120 | tf_op jit(solution)/shard_map/all_gather | solution.py:67
  181.9 321.6 %all-reduce.8.cloned.1.call-done = f32[1280,2048]{1,0:T(8,128)} async-done(((f32[1280,2048]{1,0:T(8,128)}), f32[1280,2048]{1,0:T(8,128)}) %all-reduce.8.cloned.1.call-update) | async-done | bytes 10485776 | tf_op jit(solution)/shard_map/psum | solution.py:177
  503.6 11.1 multiply_reduce_fusion
  522.0 10.8 all-gather.12.cloned.1.call-done
  532.8 9.6 fusion.161
  542.4 20.5 %all-gather.10.cloned.1.call-done = bf16[2048,768]{1,0:T(8,128)(2,1)} async-done(((bf16[512,768]{1,0:T(8,128)(2,1)}), bf16[2048,768]{1,0:T(8,128)(2,1)}) %all-gather.10.cloned.1.call-update) | async-done | bytes 3145744 | tf_op jit(solution)/shard_map/all_gather | solution.py:68
  562.9 9.7 fusion.160
  572.6 20.4 %all-gather.14.cloned.1.call-done = bf16[768,2048]{1,0:T(8,128)(2,1)} async-done(((bf16[768,512]{1,0:T(8,128)(2,1)}), bf16[768,2048]{1,0:T(8,128)(2,1)}) %all-gather.14.cloned.1.call-update) | async-done | bytes 3145744 | tf_op jit(solution)/shard_map/all_gather | solution.py:70
  592.9 13.6 multiply_convert_fusion.1
  619.2 183.7 %all-reduce.10.cloned.1.call-done = bf16[1280,2048]{1,0:T(8,128)(2,1)} async-done(((bf16[1280,2048]{1,0:T(8,128)(2,1)}), bf16[1280,2048]{1,0:T(8,128)(2,1)}) %all-reduce.10.cloned.1.call-update) | async-done | bytes 5242896 | tf_op jit(solution)/shard_map/psum | solution.py:197
  802.9 9.4 fusion.124
  824.3 8.2 conditional.24
  832.8 13.0 conditional.28
  855.9 8.2 convolution_convert_fusion.1
  864.4 9.1 convolution_convert_fusion.2
  873.6 9.1 convolution_convert_fusion.3
  901.5 44.9 %reduce-scatter.10.cloned.1.call-done = bf16[1280,256]{0,1:T(8,128)(2,1)} async-done(((bf16[5120,256]{0,1:T(8,128)(2,1)}), bf16[1280,256]{0,1:T(8,128)(2,1)}) %reduce-scatter.10.cloned.1.call-update) | async-done | bytes 655376 | tf_op jit(solution)/shard_map/reduce_scatter | solution.py:242
  983.1 13.4 add_convert_fusion
  1001.0 26.6 %reduce-scatter.24.cloned.1.call-done = bf16[512,768]{1,0:T(8,128)(2,1)} async-done(((bf16[2048,768]{1,0:T(8,128)(2,1)}), bf16[512,768]{1,0:T(8,128)(2,1)}) %reduce-scatter.24.cloned.1.call-update) | async-done | bytes 786448 | tf_op jit(solution)/shard_map/reduce_scatter | solution.py:300
  1030.0 38.0 %reduce-scatter.22.cloned.1.call-done = bf16[512,768]{1,0:T(8,128)(2,1)} async-done(((bf16[2048,768]{1,0:T(8,128)(2,1)}), bf16[512,768]{1,0:T(8,128)(2,1)}) %reduce-scatter.22.cloned.1.call-update) | async-done | bytes 786448 | tf_op jit(solution)/shard_map/reduce_scatter | solution.py:297
  1070.4 22.0 %reduce-scatter.20.cloned.1.call-done = bf16[128,512]{1,0:T(8,128)(2,1)} async-done(((bf16[128,2048]{1,0:T(8,128)(2,1)}), bf16[128,512]{1,0:T(8,128)(2,1)}) %reduce-scatter.20.cloned.1.call-update) | async-done | bytes 131088 | tf_op jit(solution)/shard_map/reduce_scatter | solution.py:291
  1094.0 22.4 %reduce-scatter.18.cloned.1.call-done = bf16[512,128]{1,0:T(8,128)(2,1)} async-done(((bf16[2048,128]{1,0:T(8,128)(2,1)}), bf16[512,128]{1,0:T(8,128)(2,1)}) %reduce-scatter.18.cloned.1.call-update) | async-done | bytes 131088 | tf_op jit(solution)/shard_map/reduce_scatter | solution.py:288
  1118.0 22.7 %reduce-scatter.12.cloned.1.call-done = bf16[512,128]{1,0:T(8,128)(2,1)} async-done(((bf16[2048,128]{1,0:T(8,128)(2,1)}), bf16[512,128]{1,0:T(8,128)(2,1)}) %reduce-scatter.12.cloned.1.call-update) | async-done | bytes 131088 | tf_op jit(solution)/shard_map/reduce_scatter | solution.py:279
  1142.4 20.8 %reduce-scatter.16.cloned.1.call-done = bf16[512,64]{0,1:T(8,128)(2,1)} async-done(((bf16[2048,64]{0,1:T(8,128)(2,1)}), bf16[512,64]{0,1:T(8,128)(2,1)}) %reduce-scatter.16.cloned.1.call-update) | async-done | bytes 65552 | tf_op jit(solution)/shard_map/reduce_scatter | solution.py:285
  1164.7 21.0 %reduce-scatter.14.cloned.1.call-done = bf16[512,64]{0,1:T(8,128)(2,1)} async-done(((bf16[2048,64]{0,1:T(8,128)(2,1)}), bf16[512,64]{0,1:T(8,128)(2,1)}) %reduce-scatter.14.cloned.1.call-update) | async-done | bytes 65552 | tf_op jit(solution)/shard_map/reduce_scatter | solution.py:282
  1187.2 331.0 %all-reduce.12.cloned.1.call-done = (bf16[1280,2048]{1,0:T(8,128)(2,1)}, bf16[1280,2048]{1,0:T(8,128)(2,1)}) async-done(((bf16[1280,2048]{1,0:T(8,128)(2,1)}, bf16[1280,2048]{1,0:T(8,128)(2,1)}), (bf16[1280,2048]{1,0:T(8,128)(2,1)}, bf16[1280,2048]{1,0:T(8,128)(2,1)})) %all-reduce.12.cloned.1.call-update) | async-done | bytes 10485776 | tf_op jit(solution)/shard_map/psum | solution.py:195
  1518.2 10.0 add_convert_fusion.2
  1543.9 19.1 %psum.40 = bf16[512]{0:T(512)(128)(2,1)S(1)} all-reduce(bf16[512]{0:T(512)(128)(2,1)S(1)} %dynamic-slice.3), channel_id=1, replica_groups=mesh['batch'=4,'head'=8] {'head'}, use_global_device_ids=true, to_apply=%region_61.62 | all-reduce | flops 512 | bytes 2048 | tf_op jit(solution)/shard_map/psum | solution.py:266
  1563.6 10.8 fusion.119
  (209 shorter events, 252.7 us)
Async XLA Ops:
  7.2 85.5 %all-gather.8.cloned.1.call-start = ((), (), s32[]{:S(2)}) async-start(), calls=%async_computation.9 | async-start | bytes 3276800 | tf_op jit(solution)/shard_map/all_gather | solution.py:112
  7.2 23.8 %copy-start.2 = (bf16[1280,2048]{1,0:T(8,128)(2,1)S(1)}, bf16[1280,2048]{1,0:T(8,128)(2,1)}, u32[]{:S(2)}) copy-start(bf16[1280,2048]{1,0:T(8,128)(2,1)} %param.45) | copy-start | bytes 15728644
  14.3 18.0 %copy-start.21 = (f32[4,1,512]{2,1,0:T(1,128)}, f32[4,1,512]{2,1,0:T(1,128)S(1)}, u32[]{:S(2)}) copy-start(f32[4,1,512]{2,1,0:T(1,128)S(1)} %convert_element_type.276) | copy-start | bytes 24580
  18.5 18.0 %copy-start.23 = (f32[1280]{0:T(1024)}, f32[1280]{0:T(1024)S(1)}, u32[]{:S(2)}) copy-start(f32[1280]{0:T(1024)S(1)} %get-tuple-element.735) | copy-start | bytes 15364
  25.0 11.6 copy-start.17
  34.6 13.1 copy-start.20
  34.7 27.8 %copy-start.25 = (bf16[512,128]{1,0:T(8,128)(2,1)S(1)}, bf16[512,128]{1,0:T(8,128)(2,1)}, u32[]{:S(2)}) copy-start(bf16[512,128]{1,0:T(8,128)(2,1)} %param.48) | copy-start | bytes 393220
  34.7 38.2 %copy-start.26 = (bf16[512,128]{1,0:T(8,128)(2,1)S(1)}, bf16[512,128]{1,0:T(8,128)(2,1)}, u32[]{:S(2)}) copy-start(bf16[512,128]{1,0:T(8,128)(2,1)} %param.51) | copy-start | bytes 393220
  34.7 46.0 %copy-start.27 = (bf16[128,512]{1,0:T(8,128)(2,1)S(1)}, bf16[128,512]{1,0:T(8,128)(2,1)}, u32[]{:S(2)}) copy-start(bf16[128,512]{1,0:T(8,128)(2,1)} %param.52) | copy-start | bytes 393220
  36.6 10.0 collective-permute-start
  47.7 455.9 %all-reduce.8.cloned.1.call-start = ((), (), s32[]{:S(2)}) async-start(), calls=%async_computation.10 | async-start | bytes 20971520 | tf_op jit(solution)/shard_map/psum | solution.py:177
  72.9 15.0 copy-start.11
  111.1 11.6 copy-start.5
  122.7 410.1 %all-gather.12.cloned.1.call-start = ((), (), s32[]{:S(2)}) async-start(), calls=%async_computation.12 | async-start | bytes 3932160 | tf_op jit(solution)/shard_map/all_gather | solution.py:69
  123.5 439.4 %all-gather.10.cloned.1.call-start = ((), (), s32[]{:S(2)}) async-start(), calls=%async_computation.11 | async-start | bytes 3932160 | tf_op jit(solution)/shard_map/all_gather | solution.py:68
  124.0 468.9 %all-gather.14.cloned.1.call-start = ((), (), s32[]{:S(2)}) async-start(), calls=%async_computation.13 | async-start | bytes 3932160 | tf_op jit(solution)/shard_map/all_gather | solution.py:70
  124.6 678.3 %all-reduce.10.cloned.1.call-start = ((), (), s32[]{:S(2)}) async-start(), calls=%async_computation.14 | async-start | bytes 10485760 | tf_op jit(solution)/shard_map/psum | solution.py:197
  592.9 13.6 copy-start.32
  618.7 327.7 %reduce-scatter.10.cloned.1.call-start = ((), (), s32[]{:S(2)}) async-start(), calls=%async_computation.15 | async-start | bytes 3276800 | tf_op jit(solution)/shard_map/reduce_scatter | solution.py:242
  855.8 142.7 %reduce-scatter.26.cloned.1.call-start = ((), (), s32[]{:S(2)}) async-start(), calls=%async_computation.23 | async-start | bytes 3932160 | tf_op jit(solution)/shard_map/reduce_scatter | solution.py:303
  864.2 163.5 %reduce-scatter.24.cloned.1.call-start = ((), (), s32[]{:S(2)}) async-start(), calls=%async_computation.22 | async-start | bytes 3932160 | tf_op jit(solution)/shard_map/reduce_scatter | solution.py:300
  873.5 194.5 %reduce-scatter.22.cloned.1.call-start = ((), (), s32[]{:S(2)}) async-start(), calls=%async_computation.21 | async-start | bytes 3932160 | tf_op jit(solution)/shard_map/reduce_scatter | solution.py:297
  882.7 209.7 %reduce-scatter.20.cloned.1.call-start = ((), (), s32[]{:S(2)}) async-start(), calls=%async_computation.20 | async-start | bytes 655360 | tf_op jit(solution)/shard_map/reduce_scatter | solution.py:291
  888.5 227.9 %reduce-scatter.18.cloned.1.call-start = ((), (), s32[]{:S(2)}) async-start(), calls=%async_computation.19 | async-start | bytes 655360 | tf_op jit(solution)/shard_map/reduce_scatter | solution.py:288
  893.4 247.3 %reduce-scatter.12.cloned.1.call-start = ((), (), s32[]{:S(2)}) async-start(), calls=%async_computation.16 | async-start | bytes 655360 | tf_op jit(solution)/shard_map/reduce_scatter | solution.py:279
  901.5 51.5 %copy-start.12 = (bf16[2048,128]{1,0:T(8,128)(2,1)S(1)}, bf16[2048,128]{1,0:T(8,128)(2,1)}, u32[]{:S(2)}) copy-start(bf16[2048,128]{1,0:T(8,128)(2,1)} %copy-done.11) | copy-start | bytes 1572868
  946.4 16.7 %collective-permute-start.1 = (bf16[1280,256]{0,1:T(8,128)(2,1)}, bf16[1280,256]{0,1:T(8,128)(2,1)S(1)}, u32[]{:S(2)}, u32[]{:S(2)}) collective-permute-start(bf16[1280,256]{0,1:T(8,128)(2,1)} %reduce-scatter.10.cloned.1.call-done), channel_id=1, source_target_pairs={{0,1},{1,0},{2,3},{3,2},{4,5},{5,4},{6,7},{7,6},{8,9},{9,8},{10,11... | collective-permute-start | bytes 1966088 | tf_op jit(solution)/shard_map/ppermute | solution.py:18
  952.9 10.2 copy-start.19
  952.9 210.2 %reduce-scatter.16.cloned.1.call-start = ((), (), s32[]{:S(2)}) async-start(), calls=%async_computation.18 | async-start | bytes 327680 | tf_op jit(solution)/shard_map/reduce_scatter | solution.py:285
  972.9 212.8 %reduce-scatter.14.cloned.1.call-start = ((), (), s32[]{:S(2)}) async-start(), calls=%async_computation.17 | async-start | bytes 327680 | tf_op jit(solution)/shard_map/reduce_scatter | solution.py:282
  982.8 535.4 %all-reduce.12.cloned.1.call-start = ((), (), s32[]{:S(2)}) async-start(), calls=%async_computation.24 | async-start | bytes 20971520 | tf_op jit(solution)/shard_map/psum | solution.py:195
  1528.2 35.3 %copy-start.28 = (f32[1280]{0:T(1024)S(1)}, f32[1280]{0:T(1024)}, u32[]{:S(2)}) copy-start(f32[1280]{0:T(1024)} %get-tuple-element.734) | copy-start | bytes 15364
  (23 other events, 127.6 us)
Sparse Core Ops, SparseCore 0:
  47.8 29.6 all-gather.7
  122.9 380.6 all-reduce.7
  505.2 27.5 all-gather.11
  534.3 28.5 all-gather.9
  564.4 28.5 all-gather.13
  618.9 184.0 all-reduce.9
  855.9 90.4 reduce-scatter.9
  948.9 37.9 reduce-scatter.25
  989.6 37.9 reduce-scatter.23
  1030.0 37.9 reduce-scatter.21
  1070.7 21.6 reduce-scatter.19
  1094.7 21.6 reduce-scatter.17
  1119.1 21.6 reduce-scatter.11
  1143.1 20.0 reduce-scatter.15
  1165.6 20.0 reduce-scatter.13
  1190.2 327.9 all-reduce.11
where the time goes:
time: 1590 us; the launch traced here: 1580 us
  waiting for transfers between devices  1120 us (70%)
  matrix products  175 us (11%)
  blocking collectives  133 us (8%)
  other arithmetic  95.2 us (6%)
  local copies, waits for them, and re-layouts  25 us (2%)
  between operations  23.4 us (1%)
    psum x1, waiting for transfers between devices, per_device(): lax.psum(mlp_part.astype(jnp.bfloat16), 'head').astype(jnp.float32)  331 us
    psum x1, waiting for transfers between devices, per_device(): resid = inputs + lax.psum(attn_part, 'head')  322 us
    psum x1, waiting for transfers between devices, per_device(): lax.psum(dn2_part.astype(jnp.bfloat16), 'head').astype(jnp.float32)  184 us
    dot_general x13, matrix products, cols_inner(): lax.dot_general(left, right, (((1,), (1,)), ((), ())), preferred_element_...  73.1 us
    all_gather x1, blocking collectives, per_device(): lax.all_gather(norm2_gain, 'batch', axis=0, tiled=True)  57.2 us
    dot_general x10, matrix products, rows_inner(): lax.dot_general(left, right, (((0,), (0,)), ((), ())), preferred_element_...  51.8 us
    dot_general x9, matrix products, matmul(): return jnp.dot(left, right, preferred_element_type=jnp.float32)  50.3 us
    reduce_scatter x1, waiting for transfers between devices, per_device(): lax.psum_scatter(d_kv_all.astype(jnp.bfloat16), 'batch', scatter_dimensio...  44.9 us
  transfers between devices with their start and end apart: 18, of which 16 were waited for; matrix products, arithmetic and copies ran while one was open for 9% of the time, Pallas kernels for 0%

commit v1 on v0

--- a/solution.py
+++ b/solution.py
@@ -174,7 +174,7 @@
     gate_vals = jax.nn.sigmoid(matmul(normed_one, gate_full))
     mixed = (attended * gate_vals).astype(jnp.bfloat16)
     attn_part = matmul(mixed, out_full)
-    resid = inputs + lax.psum(attn_part, "head")
+    resid = inputs + jnp.sum(lax.all_gather(attn_part, "head"), axis=0)
     recip_two = rms_scale(resid)
     normed_two = (resid * recip_two * gain_two).astype(jnp.bfloat16)
     gate_pre = matmul(normed_two, mgate_full)

time: 1590 us -> 2850 us (1.79)
  waiting for transfers between devices: 1120 us -> 2340 us
  other arithmetic: 95.2 us -> 127 us
    all_gather x0 -> x1, waiting for transfers between devices: none -> 1580 us  [per_device(): resid = inputs + jnp.sum(lax.all_gather(attn_part, 'head'), axis=0)]
    psum x1 -> x0, waiting for transfers between devices: 322 us -> none  [per_device(): resid = inputs + lax.psum(attn_part, 'head')]
    reduce_scatter x1, waiting for transfers between devices: 0.02 us -> 38.9 us  [per_device(): lax.psum_scatter(d_down.astype(jnp.bfloat16), 'batch', scatter_dimension=...]
    reduce_scatter x1, waiting for transfers between devices: 38 us -> 0.02 us  [per_device(): lax.psum_scatter(d_mgate.astype(jnp.bfloat16), 'batch', scatter_dimension...]
    reduce_sum x0 -> x1, other arithmetic: none -> 31.7 us  [per_device(): resid = inputs + jnp.sum(lax.all_gather(attn_part, 'head'), axis=0)]
  transfers between devices with their start and end apart: 18 -> 18, of which waited for: 16 -> 14; matrix products, arithmetic and copies ran while one was open for 9% -> 6% of each run, Pallas kernels for 0% -> 0%
where the time goes in v1:
time: 2850 us; the launch traced here: 2840 us
  waiting for transfers between devices  2340 us (82%)
  matrix products  176 us (6%)
  blocking collectives  132 us (5%)
  other arithmetic  127 us (4%)
    all_gather x1, waiting for transfers between devices, per_device(): resid = inputs + jnp.sum(lax.all_gather(attn_part, 'head'), axis=0)  1580 us
    psum x1, waiting for transfers between devices, per_device(): lax.psum(mlp_part.astype(jnp.bfloat16), 'head').astype(jnp.float32)  332 us
    psum x1, waiting for transfers between devices, per_device(): lax.psum(dn2_part.astype(jnp.bfloat16), 'head').astype(jnp.float32)  184 us
    dot_general x13, matrix products, cols_inner(): lax.dot_general(left, right, (((1,), (1,)), ((), ())), preferred_element_...  72.6 us
    all_gather x1, blocking collectives, per_device(): lax.all_gather(norm2_gain, 'batch', axis=0, tiled=True)  57 us
  transfers between devices with their start and end apart: 18, of which 14 were waited for; matrix products, arithmetic and copies ran while one was open for 6% of the time, Pallas kernels for 0%

profile of v1, /device:TPU:0, one launch (start us, length us, event | category | flops | bytes accessed | tf_op | source)
XLA Modules:
  0.0 2835.1 jit_solution(5410276101814420701)
XLA Ops:
  38.2 8.3 collective-permute-done
  62.3 10.5 all_gather.47
  92.6 9.2 conditional.16
  124.3 57.0 %all-gather.3 = bf16[4,1,512]{2,1,0:T(2,128)(2,1)S(1)} all-gather(bf16[1,1,512]{2,1,0:T(2,128)(2,1)S(1)} %reshape.213), channel_id=1, replica_groups=mesh['batch'=4,'head'=8] {'batch'}, dimensions={0}, use_global_device_ids=true | all-gather | bytes 5120 | tf_op jit(solution)/shard_map/all_gather | solution.py:67
  181.3 1576.0 %all-gather.18.cloned.1.call-done = f32[10240,2048]{1,0:T(8,128)} async-done(((f32[1280,2048]{1,0:T(8,128)}), f32[10240,2048]{1,0:T(8,128)}) %all-gather.18.cloned.1.call-update) | async-done | bytes 83886096 | tf_op jit(solution)/shard_map/all_gather | solution.py:177
  1757.3 31.7 %reduce_sum.136 = f32[1280,2048]{1,0:T(8,128)} reduce(f32[8,1280,2048]{2,1,0:T(8,128)} %bitcast.6, f32[]{:T(128)} %constant.167.clone.1), dimensions={0}, to_apply=%region_25.26 | reduce | flops 18350080 | bytes 94371840 | tf_op jit(solution)/shard_map/reduce_sum | solution.py:177
  1789.1 10.9 multiply_reduce_fusion
  1807.2 9.6 fusion.160
  1817.4 9.6 fusion.161
  1827.0 20.4 all-gather.16.cloned.1.call-done
  1847.4 13.6 multiply_convert_fusion.1
  1873.2 184.1 %all-reduce.7.cloned.1.call-done = bf16[1280,2048]{1,0:T(8,128)(2,1)} async-done(((bf16[1280,2048]{1,0:T(8,128)(2,1)}), bf16[1280,2048]{1,0:T(8,128)(2,1)}) %all-reduce.7.cloned.1.call-update) | async-done | bytes 5242896 | tf_op jit(solution)/shard_map/psum | solution.py:197
  2057.4 9.4 fusion.124
  2079.0 8.2 conditional.24
  2087.7 12.9 conditional.28
  2110.1 8.4 convolution_convert_fusion.3
  2118.6 9.2 convolution_convert_fusion.2
  2144.1 9.0 convolution_convert_fusion.1
  2153.2 46.7 %reduce-scatter.10.cloned.1.call-done = bf16[1280,256]{0,1:T(8,128)(2,1)} async-done(((bf16[5120,256]{0,1:T(8,128)(2,1)}), bf16[1280,256]{0,1:T(8,128)(2,1)}) %reduce-scatter.10.cloned.1.call-update) | async-done | bytes 655376 | tf_op jit(solution)/shard_map/reduce_scatter | solution.py:242
  2201.4 9.1 convolution_convert_fusion
  2237.0 13.4 add_convert_fusion
  2254.8 26.3 reduce-scatter.24.cloned.1.call-done
  2283.5 21.8 reduce-scatter.20.cloned.1.call-done
  2306.9 22.6 reduce-scatter.12.cloned.1.call-done
  2331.1 22.5 reduce-scatter.18.cloned.1.call-done
  2355.2 38.9 %reduce-scatter.26.cloned.1.call-done = bf16[768,512]{1,0:T(8,128)(2,1)} async-done(((bf16[768,2048]{1,0:T(8,128)(2,1)}), bf16[768,512]{1,0:T(8,128)(2,1)}) %reduce-scatter.26.cloned.1.call-update) | async-done | bytes 786448 | tf_op jit(solution)/shard_map/reduce_scatter | solution.py:303
  2396.6 20.1 reduce-scatter.14.cloned.1.call-done
  2418.2 20.8 reduce-scatter.16.cloned.1.call-done
  2440.5 331.6 %all-reduce.9.cloned.1.call-done = (bf16[1280,2048]{1,0:T(8,128)(2,1)}, bf16[1280,2048]{1,0:T(8,128)(2,1)}) async-done(((bf16[1280,2048]{1,0:T(8,128)(2,1)}, bf16[1280,2048]{1,0:T(8,128)(2,1)}), (bf16[1280,2048]{1,0:T(8,128)(2,1)}, bf16[1280,2048]{1,0:T(8,128)(2,1)})) %all-reduce.9.cloned.1.call-update) | async-done | bytes 10485776 | tf_op jit(solution)/shard_map/psum | solution.py:195
  2787.1 19.1 psum.32
  2807.4 10.0 add_convert_fusion.2
  2817.5 10.9 fusion.119
  (210 shorter events, 240.2 us)
Async XLA Ops:
  7.2 85.4 %all-gather.10.cloned.1.call-start = ((), (), s32[]{:S(2)}) async-start(), calls=%async_computation.9 | async-start | bytes 3276800 | tf_op jit(solution)/shard_map/all_gather | solution.py:112
  7.2 23.7 copy-start.2
  11.6 24.9 copy-start.21
  18.4 18.1 copy-start.23
  24.8 11.6 copy-start.17
  34.5 13.1 copy-start.20
  34.5 27.8 copy-start.25
  34.5 38.3 %copy-start.26 = (bf16[512,128]{1,0:T(8,128)(2,1)S(1)}, bf16[512,128]{1,0:T(8,128)(2,1)}, u32[]{:S(2)}) copy-start(bf16[512,128]{1,0:T(8,128)(2,1)} %param.51) | copy-start | bytes 393220
  34.5 46.0 %copy-start.27 = (bf16[128,512]{1,0:T(8,128)(2,1)S(1)}, bf16[128,512]{1,0:T(8,128)(2,1)}, u32[]{:S(2)}) copy-start(bf16[128,512]{1,0:T(8,128)(2,1)} %param.52) | copy-start | bytes 393220
  36.5 10.0 collective-permute-start
  47.6 1709.7 %all-gather.18.cloned.1.call-start = ((), (), s32[]{:S(2)}) async-start(), calls=%async_computation.23 | async-start | bytes 94371840 | tf_op jit(solution)/shard_map/all_gather | solution.py:177
  72.8 19.7 copy-start.11
  110.7 11.6 copy-start.5
  122.3 1684.9 %all-gather.12.cloned.1.call-start = ((), (), s32[]{:S(2)}) async-start(), calls=%async_computation.10 | async-start | bytes 3932160 | tf_op jit(solution)/shard_map/all_gather | solution.py:68
  123.1 1694.3 %all-gather.14.cloned.1.call-start = ((), (), s32[]{:S(2)}) async-start(), calls=%async_computation.11 | async-start | bytes 3932160 | tf_op jit(solution)/shard_map/all_gather | solution.py:69
  123.7 1723.7 %all-gather.16.cloned.1.call-start = ((), (), s32[]{:S(2)}) async-start(), calls=%async_computation.12 | async-start | bytes 3932160 | tf_op jit(solution)/shard_map/all_gather | solution.py:70
  124.2 1933.1 %all-reduce.7.cloned.1.call-start = ((), (), s32[]{:S(2)}) async-start(), calls=%async_computation.13 | async-start | bytes 10485760 | tf_op jit(solution)/shard_map/psum | solution.py:197
  1847.4 13.6 copy-start.31
  1873.2 326.7 %reduce-scatter.10.cloned.1.call-start = ((), (), s32[]{:S(2)}) async-start(), calls=%async_computation.14 | async-start | bytes 3276800 | tf_op jit(solution)/shard_map/reduce_scatter | solution.py:242
  2105.7 146.7 %reduce-scatter.22.cloned.1.call-start = ((), (), s32[]{:S(2)}) async-start(), calls=%async_computation.20 | async-start | bytes 3932160 | tf_op jit(solution)/shard_map/reduce_scatter | solution.py:297
  2118.6 162.5 %reduce-scatter.24.cloned.1.call-start = ((), (), s32[]{:S(2)}) async-start(), calls=%async_computation.21 | async-start | bytes 3932160 | tf_op jit(solution)/shard_map/reduce_scatter | solution.py:300
  2127.8 177.4 %reduce-scatter.20.cloned.1.call-start = ((), (), s32[]{:S(2)}) async-start(), calls=%async_computation.19 | async-start | bytes 655360 | tf_op jit(solution)/shard_map/reduce_scatter | solution.py:291
  2133.6 195.9 %reduce-scatter.12.cloned.1.call-start = ((), (), s32[]{:S(2)}) async-start(), calls=%async_computation.15 | async-start | bytes 655360 | tf_op jit(solution)/shard_map/reduce_scatter | solution.py:279
  2138.7 214.9 %reduce-scatter.18.cloned.1.call-start = ((), (), s32[]{:S(2)}) async-start(), calls=%async_computation.18 | async-start | bytes 655360 | tf_op jit(solution)/shard_map/reduce_scatter | solution.py:288
  2143.7 250.4 %reduce-scatter.26.cloned.1.call-start = ((), (), s32[]{:S(2)}) async-start(), calls=%async_computation.22 | async-start | bytes 3932160 | tf_op jit(solution)/shard_map/reduce_scatter | solution.py:303
  2153.1 57.3 %copy-start.12 = (bf16[2048,128]{1,0:T(8,128)(2,1)S(1)}, bf16[2048,128]{1,0:T(8,128)(2,1)}, u32[]{:S(2)}) copy-start(bf16[2048,128]{1,0:T(8,128)(2,1)} %copy-done.11) | copy-start | bytes 1572868
  2153.1 263.5 %reduce-scatter.14.cloned.1.call-start = ((), (), s32[]{:S(2)}) async-start(), calls=%async_computation.16 | async-start | bytes 327680 | tf_op jit(solution)/shard_map/reduce_scatter | solution.py:282
  2199.9 17.2 collective-permute-start.1
  2227.0 212.0 %reduce-scatter.16.cloned.1.call-start = ((), (), s32[]{:S(2)}) async-start(), calls=%async_computation.17 | async-start | bytes 327680 | tf_op jit(solution)/shard_map/reduce_scatter | solution.py:285
  2237.0 535.1 %all-reduce.9.cloned.1.call-start = ((), (), s32[]{:S(2)}) async-start(), calls=%async_computation.24 | async-start | bytes 20971520 | tf_op jit(solution)/shard_map/psum | solution.py:195
  2250.5 521.6 %copy-start.22 = (f32[1280]{0:T(1024)S(1)}, f32[1280]{0:T(1024)}, u32[]{:S(2)}) copy-start(f32[1280]{0:T(1024)} %copy-done.21) | copy-start | bytes 15364
  2250.5 521.6 %copy-start.24 = (f32[4,1,512]{2,1,0:T(1,128)S(1)}, f32[4,1,512]{2,1,0:T(1,128)}, u32[]{:S(2)}) copy-start(f32[4,1,512]{2,1,0:T(1,128)} %copy-done.23) | copy-start | bytes 24580
  (23 other events, 122.6 us)
Sparse Core Ops, SparseCore 0:
  47.7 29.6 all-gather.9
  122.5 1634.8 all-gather.17
  1758.9 28.4 all-gather.11
  1788.8 28.5 all-gather.13
  1818.8 28.5 all-gather.15
  1873.3 184.0 all-reduce.6
  2105.8 94.0 reduce-scatter.9
  2202.6 37.9 reduce-scatter.21
  2243.1 37.9 reduce-scatter.23
  2283.6 21.6 reduce-scatter.19
  2307.7 21.6 reduce-scatter.11
  2331.9 21.6 reduce-scatter.17
  2356.1 37.9 reduce-scatter.25
  2396.6 20.0 reduce-scatter.13
  2419.0 20.0 reduce-scatter.15
  2444.0 327.9 all-reduce.8
